TPU v7x, 32 devices: a whole 2x2x4 slice. The times are simulated.
32 devices in a mesh: dp: 8 (over z, x), segment: 2 (over y), mp: 2 (over core).
Axes of the slice: x: 2, y: 2, z: 4, core: 2. Of those that a mesh axis runs over, the one named last changes fastest.
Arguments:
- prefix_hidden: bfloat16 [16, 512, 8192], P(('dp', 'segment'), 'mp'), may hold values from -6 to 6
- norm_gain: float32 [8192], replicated, may hold values from 0.5 to 1.5
- kv_weight: bfloat16 [8192, 2, 1024], P('dp', None, 'mp'), may hold values from -0.0625 to 0.0625
- action_query: bfloat16 [16, 128, 2048], P(('dp', 'segment'), None, 'mp'), may hold values from -104 to 104
- action_kv: bfloat16 [16, 128, 2, 1024], P(('dp', 'segment'), None, None, 'mp'), may hold values from -4.25 to 4.25
- out_cotangent: bfloat16 [16, 128, 2048], P(('dp', 'segment'), None, 'mp'), may hold values from -18 to 18
- prefix_blocks: int32 [16, 512], P(('dp', 'segment')), may hold values from 0 to 7, as said below
- action_blocks: int32 [16, 128], P(('dp', 'segment')), may hold values from 0 to 8, as said below
- prefix_lengths: int32 [16], P(('dp', 'segment')), may hold values from 128 to 512, as said below
- timesteps: int32 [16], P(('dp', 'segment')), may hold values from 0 to 999
Outputs:
- attn_out: bfloat16 [16, 128, 2048], P(('dp', 'segment'), None, 'mp')
- query_grad: float32 [16, 128, 2048], P(('dp', 'segment'), None, 'mp')
- action_kv_grad: float32 [16, 128, 2, 1024], P(('dp', 'segment'), None, None, 'mp')
- weight_grad: float32 [8192, 2, 1024], P('dp', None, 'mp')
Inputs may be any that keep to these rules, and one draw needn't show every extreme that they name: `prefix_blocks`: constant over each run of 64 positions, 0 on the first run, rising by 0 or 1 from one run to the next; in every draw some sample rises at every run. `action_blocks`: constant over each run of 64 positions; the last run of every sample holds 8; in every draw some sample's first run holds 0. `prefix_lengths`: in every draw some sample's prefix is whole and some sample's is 128.
All inputs are finite; a program needn't handle non-finite values.
Results may differ from a plain program's by a relative error of at most 0.017.
Values may be sent and summed in bfloat16 or wider, within the bound.
A program may use at most 128 MiB of HBM per device.

v0:
```python
import functools

import jax
import jax.numpy as jnp
from jax import lax
from jax.experimental import pallas as pl
from jax.experimental.pallas import tpu as pltpu
from jax.sharding import PartitionSpec as P

KVH = 8
HD = 128
QH = 16
STEPS = 1000


EPS = 1e-06
NEGATIVE = -1e30
CHUNKS = 4
MiB = 1 << 20


def inner_of(ndp):
    return 2 if ndp % 2 == 0 else 1


def remote(src, dst, send_sem, recv_sem, where):
    return pltpu.make_async_remote_copy(
        src_ref=src,
        dst_ref=dst,
        send_sem=send_sem,
        recv_sem=recv_sem,
        device_id=where,
        device_id_type=pl.DeviceIdType.MESH,
    )


def greet(peers):
    barrier = pltpu.get_barrier_semaphore()
    for peer in peers:
        pl.semaphore_signal(
            barrier, inc=1, device_id=peer, device_id_type=pl.DeviceIdType.MESH
        )
    pl.semaphore_wait(barrier, len(peers))


def project_kernel(
    ndp, nmp, w_ref, n_ref, kvc_ref, n_all, w_all, acc,
    own_sem, zs, zr, xs, xr, ys, yr, ms, mr, fs, fr,
):
    nx = inner_of(ndp)
    nz = ndp // nx
    dp, seg, mp = lax.axis_index("dp"), lax.axis_index("segment"), lax.axis_index("mp")
    z, x = dp // nx, dp % nx
    z_peer = [{"dp": ((z + o) % nz) * nx + x} for o in range(1, nz)]
    x_peer = {"dp": z * nx + (nx - 1 - x)}
    y_peer = {"segment": 1 - seg}
    m_peer = [{"mp": (mp + o) % nmp} for o in range(1, nmp)]
    greet(z_peer + ([x_peer] if nx > 1 else []) + [y_peer] + m_peer)
    depth = w_ref.shape[0]
    step = depth // CHUNKS
    mine, theirs = seg * nmp + mp, (1 - seg) * nmp + mp
    order = [0] + sorted(range(1, nz), key=lambda o: min(o, nz - o))

    def outer(o):
        return (z + nz - o) % nz

    def columns(o):
        return pl.ds(pl.multiple_of(outer(o) * (nx * depth), nx * depth), nx * depth)

    def z_copy(o, c):
        part = pl.ds(c * step, step)
        return remote(w_ref.at[part], w_all.at[dp, part], zs.at[o - 1, c], zr.at[o - 1, c], z_peer[o - 1])

    def x_copy(o, c):
        part = pl.ds(c * step, step)
        src = outer(o) * nx + x
        held = w_ref.at[part] if o == 0 else w_all.at[src, part]
        return remote(held, w_all.at[src, part], xs.at[o, c], xr.at[o, c], x_peer)

    def y_copy(o):
        return remote(n_ref.at[:, columns(o)], n_all.at[mine, :, columns(o)], ys.at[o], yr.at[o], y_peer)

    def m_copy(p):
        return remote(n_ref, n_all.at[mine], ms.at[p], mr.at[p], m_peer[p])

    def f_copy(o, p):
        part = n_all.at[theirs, :, columns(o)]
        return remote(part, part, fs.at[o, p], fr.at[o, p], m_peer[p])

    own_w = pltpu.make_async_copy(w_ref, w_all.at[dp], own_sem.at[0])
    own_n = pltpu.make_async_copy(n_ref, n_all.at[mine], own_sem.at[1])
    for o in order[1:]:
        for c in range(CHUNKS):
            z_copy(o, c).start()
    if nx > 1:
        for c in range(CHUNKS):
            x_copy(0, c).start()
    for o in order:
        y_copy(o).start()
    for p in range(nmp - 1):
        m_copy(p).start()
    own_w.start()
    own_n.start()
    acc[...] = jnp.zeros_like(acc)

    def multiply(block):
        cols = pl.ds(pl.multiple_of(block * depth, depth), depth)

        @pl.loop(0, n_all.shape[0])
        def _(i):
            acc[i] += jnp.dot(n_all[i, :, cols], w_all[block], preferred_element_type=jnp.float32)

    def finish(o):
        for p in range(nmp - 1):
            f_copy(o, p).wait_recv()
        if o == 0:
            own_w.wait()
            own_n.wait()
            for p in range(nmp - 1):
                m_copy(p).wait_recv()
        multiply(outer(o) * nx + x)
        if nx > 1:
            for c in range(CHUNKS):
                x_copy(o, c).wait_recv()
            multiply(outer(o) * nx + (nx - 1 - x))

    for i, o in enumerate(order):
        if o > 0:
            for c in range(CHUNKS):
                z_copy(o, c).wait_recv()
                if nx > 1:
                    x_copy(o, c).start()
        y_copy(o).wait_recv()
        for p in range(nmp - 1):
            f_copy(o, p).start()
        if i > 0:
            finish(order[i - 1])
    finish(order[-1])
    kvc_ref[...] = acc[...].astype(kvc_ref.dtype)
    for o in order:
        if o > 0:
            for c in range(CHUNKS):
                z_copy(o, c).wait_send()
        if nx > 1:
            for c in range(CHUNKS):
                x_copy(o, c).wait_send()
        y_copy(o).wait_send()
        for p in range(nmp - 1):
            f_copy(o, p).wait_send()
    for p in range(nmp - 1):
        m_copy(p).wait_send()


def project(ndp, nseg, nmp, weight, normed):
    nx = inner_of(ndp)
    nz = ndp // nx
    dma = pltpu.SemaphoreType.DMA
    vmem = pl.BlockSpec(memory_space=pltpu.VMEM)
    rows, width = normed.shape
    cols = weight.shape[1]
    others, further = max(nmp - 1, 1), max(nz - 1, 1)
    return pl.pallas_call(
        functools.partial(project_kernel, ndp, nmp),
        out_shape=(
            jax.ShapeDtypeStruct((nseg * nmp, rows, cols), jnp.bfloat16),
            jax.ShapeDtypeStruct((nseg * nmp, rows, width), normed.dtype),
        ),
        in_specs=[vmem, vmem],
        out_specs=(vmem, vmem),
        scratch_shapes=[
            pltpu.VMEM((ndp,) + weight.shape, weight.dtype),
            pltpu.VMEM((nseg * nmp, rows, cols), jnp.float32),
            dma((2,)),
            dma((further, CHUNKS)), dma((further, CHUNKS)),
            dma((nz, CHUNKS)), dma((nz, CHUNKS)),
            dma((nz,)), dma((nz,)),
            dma((others,)), dma((others,)),
            dma((nz, others)), dma((nz, others)),
        ],
        compiler_params=pltpu.CompilerParams(
            collective_id=0, has_side_effects=True, vmem_limit_bytes=20 * MiB
        ),
        name="project",
    )(weight, normed)


def attention_kernel(
    heads, ratio, kvc, q_ref, akv_ref, go_ref, vis_ref,
    out_ref, dq_ref, dakv_ref, g_ref, pair, grad, sems,
):
    seg = lax.axis_index("segment")
    peer = {"segment": 1 - seg}
    greet([peer])
    give = remote(kvc.at[1 - seg], pair.at[seg], sems.at[0], sems.at[1], peer)
    give.start()
    keep = pltpu.make_async_copy(kvc.at[seg], pair.at[seg], sems.at[2])
    keep.start()
    keep.wait()
    give.wait()
    acts = q_ref.shape[0]
    rows = pair.shape[1]
    scale = HD ** (-0.5)
    vis = vis_ref[...]
    visible = jnp.concatenate([vis] * ratio, axis=0) > 0.5

    def dot(a, b, ca, cb):
        return lax.dot_general(a, b, (((ca,), (cb,)), ((), ())), preferred_element_type=jnp.float32)

    for g in range(heads):
        cols = slice(g * HD, (g + 1) * HD)
        keys = jnp.concatenate([pair[0, :, cols], akv_ref[0, :, cols]], axis=0)
        values = jnp.concatenate([pair[1, :, cols], akv_ref[1, :, cols]], axis=0)
        hs = [slice((g * ratio + r) * HD, (g * ratio + r + 1) * HD) for r in range(ratio)]
        query = jnp.concatenate([q_ref[:, h] for h in hs], axis=0)
        go = jnp.concatenate([go_ref[:, h] for h in hs], axis=0)
        masked = jnp.where(visible, dot(query, keys, 1, 1) * scale, NEGATIVE)
        top = jnp.max(masked, axis=-1, keepdims=True)
        expo = jnp.where(visible, jnp.exp(masked - top), 0.0)
        probs = expo * (1.0 / jnp.sum(expo, axis=-1, keepdims=True))
        low = probs.astype(jnp.bfloat16)
        d_probs = dot(go, values, 1, 1)
        delta = jnp.sum(probs * d_probs, axis=-1, keepdims=True)
        d_scores = (probs * (d_probs - delta)).astype(jnp.bfloat16)
        out = dot(low, values, 1, 0).astype(jnp.bfloat16)
        d_query = dot(d_scores, keys, 1, 0) * scale
        for r, h in enumerate(hs):
            out_ref[:, h] = out[r * acts : (r + 1) * acts]
            dq_ref[:, h] = d_query[r * acts : (r + 1) * acts]
        d_keys = dot(d_scores, query, 0, 0) * scale
        d_values = dot(low, go, 0, 0)
        grad[0, :, cols] = d_keys[:rows].astype(jnp.bfloat16)
        grad[1, :, cols] = d_values[:rows].astype(jnp.bfloat16)
        dakv_ref[0, :, cols] = d_keys[rows:]
        dakv_ref[1, :, cols] = d_values[rows:]
    back = remote(grad.at[1 - seg], g_ref.at[seg], sems.at[3], sems.at[4], peer)
    back.start()
    local = pltpu.make_async_copy(grad.at[seg], g_ref.at[seg], sems.at[5])
    local.start()
    local.wait()
    back.wait()


def attention(heads, ratio, kvc, query, akv, grad_out, visible):
    vmem = pl.BlockSpec(memory_space=pltpu.VMEM)
    acts, width = query.shape
    return pl.pallas_call(
        functools.partial(attention_kernel, heads, ratio),
        out_shape=(
            jax.ShapeDtypeStruct((acts, width), jnp.bfloat16),
            jax.ShapeDtypeStruct((acts, width), jnp.float32),
            jax.ShapeDtypeStruct(akv.shape, jnp.float32),
            jax.ShapeDtypeStruct(kvc.shape, jnp.bfloat16),
        ),
        in_specs=[vmem] * 5,
        out_specs=(vmem,) * 4,
        scratch_shapes=[
            pltpu.VMEM(kvc.shape, jnp.bfloat16),
            pltpu.VMEM(kvc.shape, jnp.bfloat16),
            pltpu.SemaphoreType.DMA((6,)),
        ],
        compiler_params=pltpu.CompilerParams(
            collective_id=1, has_side_effects=True, vmem_limit_bytes=12 * MiB
        ),
        name="attention",
    )(kvc, query, akv, grad_out, visible)


def scatter_kernel(ndp, n_ref, g_ref, o_ref, x_send, x_buf, z_send, z_buf, xs, xr, zs, zr, ys, yr):
    nx = inner_of(ndp)
    nz = ndp // nx
    dp, seg = lax.axis_index("dp"), lax.axis_index("segment")
    z, x = dp // nx, dp % nx
    z_peer = [{"dp": ((z + o) % nz) * nx + x} for o in range(1, nz)]
    x_peer = {"dp": z * nx + (nx - 1 - x)}
    y_peer = {"segment": 1 - seg}
    greet(z_peer + ([x_peer] if nx > 1 else []) + [y_peer])
    order = sorted(range(1, nz), key=lambda o: -min(o, nz - o)) + [0]
    rows = o_ref.shape[1]
    step = min(rows, max(rows // CHUNKS, 128))
    steps = rows // step

    def part(c):
        return pl.ds(pl.multiple_of(c * step, step), step)

    def term(block, c):
        cols = pl.ds(pl.multiple_of(block * rows + c * step, step), step)
        return lax.dot_general(
            n_ref[:, cols], g_ref[...], (((0,), (0,)), ((), ())), preferred_element_type=jnp.float32
        )

    def x_copy(o, c):
        return remote(x_send.at[o, part(c)], x_buf.at[o, part(c)], xs.at[o, c], xr.at[o, c], x_peer)

    def z_copy(o, c):
        return remote(z_send.at[o, part(c)], z_buf.at[o, part(c)], zs.at[o, c], zr.at[o, c], z_peer[o - 1])

    def y_copy(c):
        return remote(o_ref.at[seg, part(c)], o_ref.at[seg, part(c)], ys.at[c], yr.at[c], y_peer)

    if nx > 1:
        for o in order:
            @pl.loop(0, steps)
            def _(c):
                x_send[o, part(c), :] = term(((z + o) % nz) * nx + (nx - 1 - x), c).astype(jnp.bfloat16)
                x_copy(o, c).start()

    for o in order:
        @pl.loop(0, steps)
        def _(c):
            total = term(((z + o) % nz) * nx + x, c)
            if nx > 1:
                x_copy(o, c).wait_recv()
                total = total + x_buf[o, part(c), :].astype(jnp.float32)
            if o > 0:
                z_send[o, part(c), :] = total.astype(jnp.bfloat16)
                z_copy(o, c).start()
            else:
                for other in order[:-1]:
                    z_copy(other, c).wait_recv()
                    total = total + z_buf[other, part(c), :].astype(jnp.float32)
                o_ref[seg, part(c), :] = total.astype(jnp.bfloat16)
                y_copy(c).start()

    @pl.loop(0, steps)
    def _(c):
        y_copy(c).wait()
        for o in order:
            if nx > 1:
                x_copy(o, c).wait_send()
            if o > 0:
                z_copy(o, c).wait_send()


def scatter(ndp, nseg, tokens, grads):
    nx = inner_of(ndp)
    nz = ndp // nx
    dma = pltpu.SemaphoreType.DMA
    vmem = pl.BlockSpec(memory_space=pltpu.VMEM)
    block = (tokens.shape[1] // ndp, grads.shape[1])
    return pl.pallas_call(
        functools.partial(scatter_kernel, ndp),
        out_shape=jax.ShapeDtypeStruct((nseg,) + block, jnp.bfloat16),
        in_specs=[vmem, vmem],
        out_specs=vmem,
        scratch_shapes=[pltpu.VMEM((nz,) + block, jnp.bfloat16)] * 4
        + [dma((nz, CHUNKS))] * 4
        + [dma((CHUNKS,))] * 2,
        compiler_params=pltpu.CompilerParams(
            collective_id=2, has_side_effects=True, vmem_limit_bytes=24 * MiB
        ),
        name="scatter",
    )(tokens, grads)


def shards(
    ndp,
    nseg,
    nmp,
    prefix_hidden,
    norm_gain,
    kv_weight,
    action_query,
    action_kv,
    out_cotangent,
    prefix_blocks,
    action_blocks,
    prefix_lengths,
    timesteps,
):
    heads_kv = kv_weight.shape[2] // HD
    ratio = QH // KVH
    columns = kv_weight.shape[2]
    seg = lax.axis_index("segment")
    wide = prefix_hidden[0].astype(jnp.float32)
    inverse = lax.rsqrt(jnp.mean(wide * wide, axis=-1, keepdims=True) + EPS)
    normed_local = (wide * inverse * norm_gain).astype(jnp.bfloat16)
    own_weight = lax.dynamic_index_in_dim(kv_weight, seg, axis=1, keepdims=False)
    kvc, tokens = project(ndp, nseg, nmp, own_weight, normed_local)
    rows = nmp * normed_local.shape[0]
    width = normed_local.shape[1]
    kvc = kvc.reshape(nseg, rows, columns)
    flow_weight = 0.5 + (timesteps[0].astype(jnp.float32) + 0.5) / STEPS
    grad_out = (flow_weight * out_cotangent[0].astype(jnp.float32)).astype(jnp.bfloat16)
    pblocks = prefix_blocks[0]
    ablocks = action_blocks[0]
    positions = jnp.arange(rows, dtype=jnp.int32)
    see_prefix = (pblocks[None, :] <= ablocks[:, None]) & (positions[None, :] < prefix_lengths[0])
    see_action = ablocks[None, :] <= ablocks[:, None]
    visible = jnp.concatenate([see_prefix, see_action], axis=1).astype(jnp.float32)
    attn_out, query_grad, d_action, grads = attention(
        heads_kv, ratio, kvc, action_query[0], action_kv[0].transpose(1, 0, 2), grad_out, visible
    )
    summed = scatter(
        ndp, nseg, tokens.reshape(nseg * rows, width), grads.reshape(nseg * rows, columns)
    )
    weight_grad = summed.transpose(1, 0, 2).astype(jnp.float32)
    return (attn_out[None], query_grad[None], d_action.transpose(1, 0, 2)[None], weight_grad)


def solution(mesh):
    placed = (
        P(("dp", "segment"), "mp", None),
        P(),
        P("dp", None, "mp"),
        P(("dp", "segment"), None, "mp"),
        P(("dp", "segment"), None, None, "mp"),
        P(("dp", "segment"), None, "mp"),
        P(("dp", "segment"), None),
        P(("dp", "segment"), None),
        P(("dp", "segment")),
        P(("dp", "segment")),
    )
    return jax.shard_map(
        functools.partial(shards, mesh.shape["dp"], mesh.shape["segment"], mesh.shape["mp"]),
        mesh=mesh,
        in_specs=placed,
        out_specs=(
            P(("dp", "segment"), None, "mp"),
            P(("dp", "segment"), None, "mp"),
            P(("dp", "segment"), None, None, "mp"),
            P("dp", None, "mp"),
        ),
        check_vma=False,
    )
```

profile of v0, /device:TPU:0, one launch (start us, length us, event | category | flops | bytes accessed | tf_op | source)
XLA Modules:
  0.0 257.9 jit_solution(8673086053616229514)
XLA Ops:
  0.6 0.0 copy-start
  0.6 1.6 copy-done
  2.2 0.0 copy-start.2
  2.2 2.2 constant_dynamic-slice_fusion
  4.4 0.0 copy-start.5
  4.4 0.3 copy.24
  4.7 0.0 copy-done.2
  4.7 0.9 fusion
  5.6 0.0 copy-done.5
  5.6 1.2 fusion.2.n_ref
  6.8 0.0 copy-start.6
  6.9 0.0 copy-start.7
  6.9 0.0 copy-start.3
  6.9 0.0 copy-start.4
  6.9 0.0 copy-start.1
  6.9 105.6 %project.1 = (bf16[4,256,512]{2,1,0:T(8,128)(2,1)S(1)}, bf16[4,256,8192]{2,1,0:T(8,128)(2,1)S(1)}) custom-call(bf16[1024,512]{1,0:T(8,128)(2,1)S(1)} %bitcast.31, bf16[256,8192]{1,0:T(8,128)(2,1)S(1)} %fusion.2.n_ref), custom_call_target="tpu_custom_call" | custom-call | tf_op jit(solution)/shard_map/project/pallas_call | solution.py:162
  113.2 0.0 copy-done.6
  113.2 0.0 copy-done.7
  113.2 0.1 compare_and_fusion
  113.3 0.1 broadcast_compare_fusion
  114.1 0.0 copy-done.3
  114.1 0.0 copy-done.4
  114.2 0.0 copy-done.1
  114.2 28.9 %attention.1 = (bf16[128,1024]{1,0:T(8,128)(2,1)S(1)}, f32[128,1024]{1,0:T(8,128)S(1)}, f32[2,128,512]{2,1,0:T(8,128)S(1)}, bf16[2,512,512]{2,1,0:T(8,128)(2,1)S(1)}) custom-call(bf16[2,512,512]{2,1,0:T(8,128)(2,1)S(1)} %bitcast.34, bf16[128,1024]{1,0:T(8,128)(2,1)S(1)} %bitcast.37, bf16[2,128,512]{2,1,0:T(8,128)(2,1)S(1)} %bitcast.33, ...), custom_call_target="tpu_custom_call" | custom-call | tf_op jit(solution)/shard_map/attention/pallas_call | solution.py:246
  143.1 106.3 %scatter.1 = bf16[2,1024,512]{2,1,0:T(8,128)(2,1)S(1)} custom-call(bf16[1024,8192]{1,0:T(8,128)(2,1)S(1)} %bitcast.30, bf16[1024,512]{1,0:T(8,128)(2,1)S(1)} %bitcast.32), custom_call_target="tpu_custom_call" | custom-call | tf_op jit(solution)/shard_map/scatter/pallas_call | solution.py:340
  249.4 0.6 convert_bitcast_fusion
  250.0 5.3 %copy.20 = f32[1024,2,512]{2,1,0:T(2,128)} copy(f32[1024,2,512]{2,0,1:T(8,128)S(1)} %convert_bitcast_fusion) | data formatting | bytes 8388608
  255.3 1.2 copy.19
  256.4 0.7 copy.30
  257.2 0.8 copy.31
  (5 shorter events, 0.1 us)
Async XLA Ops:
  0.6 1.6 copy-start
  2.2 2.5 copy-start.2
  4.4 1.2 copy-start.5
  6.8 106.3 %copy-start.6 = (s32[1,128]{1,0:T(1,128)S(1)}, s32[1,128]{1,0:T(1,128)}, u32[]{:S(2)}) copy-start(s32[1,128]{1,0:T(1,128)} %param.17) | copy-start | bytes 1540
  6.9 106.3 %copy-start.7 = (s32[1,512]{1,0:T(1,128)S(1)}, s32[1,512]{1,0:T(1,128)}, u32[]{:S(2)}) copy-start(s32[1,512]{1,0:T(1,128)} %param.16) | copy-start | bytes 6148
  6.9 107.2 %copy-start.3 = (bf16[1,128,1024]{2,1,0:T(8,128)(2,1)S(1)}, bf16[1,128,1024]{2,1,0:T(8,128)(2,1)}, u32[]{:S(2)}) copy-start(bf16[1,128,1024]{2,1,0:T(8,128)(2,1)} %param.15) | copy-start | bytes 786436
  6.9 107.3 %copy-start.4 = (bf16[1,128,2,512]{3,2,1,0:T(2,128)(2,1)S(1)}, bf16[1,128,2,512]{3,2,1,0:T(2,128)(2,1)}, u32[]{:S(2)}) copy-start(bf16[1,128,2,512]{3,2,1,0:T(2,128)(2,1)} %param.14) | copy-start | bytes 786436
  6.9 107.3 %copy-start.1 = (bf16[1,128,1024]{2,1,0:T(8,128)(2,1)S(1)}, bf16[1,128,1024]{2,1,0:T(8,128)(2,1)}, u32[]{:S(2)}) copy-start(bf16[1,128,1024]{2,1,0:T(8,128)(2,1)} %param.13) | copy-start | bytes 786436
where the time goes:
time: 258 us
  Pallas kernels  241 us (93%)
  local copies, waits for them, and re-layouts  12 us (5%)
  other arithmetic  2.98 us (1%)
    pallas_call x1, Pallas kernels, scatter(): pl.pallas_call(functools.partial(scatter_kernel, ndp), out_shape=jax.Shap...  106 us
    pallas_call x1, Pallas kernels, project(): pl.pallas_call(functools.partial(project_kernel, ndp, nmp), out_shape=(ja...  106 us
    pallas_call x1, Pallas kernels, attention(): pl.pallas_call(functools.partial(attention_kernel, heads, ratio), out_sha...  28.9 us
    unnamed x22, local copies, waits for them, and re-layouts  9.89 us

commit v1 on v0

v1 whole, which is shorter than its diff:
```python
import functools

import jax
import jax.numpy as jnp
from jax import lax
from jax.experimental import pallas as pl
from jax.experimental.pallas import tpu as pltpu
from jax.sharding import PartitionSpec as P

HD = 128
QH = 16
KVH = 8
STEPS = 1000
EPS = 1e-06
NEGATIVE = -1e30
MiB = 1 << 20
PAIR = 2 * HD


def remote(src, dst, send_sem, recv_sem, where):
    return pltpu.make_async_remote_copy(
        src_ref=src,
        dst_ref=dst,
        send_sem=send_sem,
        recv_sem=recv_sem,
        device_id=where,
        device_id_type=pl.DeviceIdType.MESH,
    )


def first_axis(chunk):
    return 1 if chunk % 4 == 1 else 0


class Plan:
    def __init__(self, nz, chunks):
        self.nz, self.chunks = nz, chunks
        self.free = dict(core=0.0, x=0.0, s=0.0, z=0.0, m=0.0)
        self.arrived = {}
        self.pending = []
        self.order = []

    def add(self, key, needs, cost, sends, rank):
        self.pending.append((key, needs, cost, sends, rank))

    def run(self):
        done = set()
        while self.pending:
            best = None
            for entry in self.pending:
                key, needs, cost, sends, rank = entry
                if any(n not in self.arrived for n in needs):
                    continue
                ready = max([self.free["core"]] + [self.arrived[n] for n in needs])
                pick = (ready, rank)
                if best is None or pick < best[0]:
                    best = (pick, entry)
            (ready, _), entry = best
            self.pending.remove(entry)
            key, needs, cost, sends, rank = entry
            self.order.append(key)
            self.arrived[key] = ready + cost
            self.free["core"] = ready + cost
            for name, link, size in sends:
                start = max(ready + cost, self.free[link])
                self.free[link] = start + size
                self.arrived[name] = start + size + 1.5
        return self.order


UNIT = 5.6


def stages(nz, chunks):
    plan = Plan(nz, chunks)
    piece = UNIT
    for c in range(chunks):
        needs = [] if c < 2 else [("wf", c - 2, nz - 1)]
        plan.add(("wo", c), needs, 0.1, [(("w", c, 1), "z", piece)], c * 0.01)
        for k in range(1, nz):
            needs = [("w", c, k)] + ([("wf", c, k - 1)] if k > 1 else [("wo", c)])
            sends = [(("w", c, k + 1), "z", piece)] if k < nz - 1 else []
            plan.add(("wf", c, k), needs, 0.1, sends, 1)
    for j in range(nz):
        needs = [("ns", j - 1)] if j else [("wo", 0)]
        plan.add(
            ("ns", j), needs, 0.1,
            [(("nx", j), "x", piece), (("ny", j), "s", piece), (("nd", j), "x", piece), (("nd2", j), "s", piece)], 0.005,
        )
        plan.add(("nf", j), [("nx", j), ("ny", j), ("nd", j), ("nd2", j)], 0.1, [(("nm", j), "m", 2.0)], 2)
    for c in range(chunks):
        one, two = ("x", "s") if first_axis(c) == 0 else ("s", "x")
        needs = [("nm", j) for j in range(nz)] + [("wf", c, k) for k in range(1, nz)]
        plan.add(("A", c), needs, 3.0, [(("p", c), one, 2 * piece)], 10 + c)
        plan.add(("B", c), [("A", c), ("p", c)], 0.5, [(("y", c), two, piece)], 7)
        plan.add(
            ("C", c), [("B", c), ("y", c)], 2.0,
            [(("g0", c), two, piece), (("g1", c), one, piece)], 6,
        )
        plan.add(("G", c), [("C", c), ("g0", c)], 0.1, [(("g2", c), one, piece)], 4)
        plan.add(("D", c), [("G", c), ("g1", c), ("g2", c)] + ([("F", c - 2)] if c >= 2 else []), 3.3, [], 9)
        for off in range(nz - 1, 0, -1):
            needs = [("D", c)] if off == nz - 1 else [("E", c, off + 1), ("e", c, off + 1)]
            plan.add(("E", c, off), needs, 0.3, [(("e", c, off), "z", piece)], 3)
        plan.add(("F", c), [("E", c, 1), ("e", c, 1)], 0.3, [(("o", c), "s", piece)], 5)
    return plan.run()


def kernel(
    order, nz, nmp, ratio,
    w_ref, n_ref, q_ref, akv_ref, go_ref, vis_ref,
    out_ref, dq_ref, dakv_ref, o_ref,
    nb, wb, keep, ps, px, ys, yb, gb, dw, zs, zb,
    w_send, w_recv, own_n, own_w, n_send, n_recv, f_send, f_recv,
    p_send, p_recv, y_send, y_recv, g_send, g_recv, z_send, z_recv, o_send, o_recv,
):
    dp, seg, mp = lax.axis_index("dp"), lax.axis_index("segment"), lax.axis_index("mp")
    z, x = dp // 2, dp % 2
    chunks, half = w_ref.shape[0], w_ref.shape[1]
    tokens = n_ref.shape[0]
    samples, rows = nb.shape[0], nb.shape[1]
    others = nmp - 1
    acts = q_ref.shape[0]
    scale = HD ** (-0.5)

    x_dp = z * 2 + (1 - x)
    plane = [
        {"dp": x_dp},
        {"segment": 1 - seg},
        {"dp": x_dp, "segment": 1 - seg},
    ]
    plane_xs = [(1 - x, seg), (x, 1 - seg), (1 - x, 1 - seg)]
    m_peer = [{"mp": (mp + o) % nmp} for o in range(1, nmp)]
    up = {"dp": (z + 1) * 2 + x}
    down = {"dp": (z - 1) * 2 + x}
    has_up, has_down = z < nz - 1, z > 0
    mine = x * 2 + seg

    barrier = pltpu.get_barrier_semaphore()
    for peer in plane + m_peer:
        pl.semaphore_signal(barrier, inc=1, device_id=peer, device_id_type=pl.DeviceIdType.MESH)

    @pl.when(has_up)
    def _():
        pl.semaphore_signal(barrier, inc=1, device_id=up, device_id_type=pl.DeviceIdType.MESH)

    @pl.when(has_down)
    def _():
        pl.semaphore_signal(barrier, inc=1, device_id=down, device_id_type=pl.DeviceIdType.MESH)

    ends = has_up.astype(jnp.int32) + has_down.astype(jnp.int32)
    pl.semaphore_wait(barrier, len(plane) + len(m_peer) + ends)

    def block(b):
        return pl.ds(pl.multiple_of(b * half, half), half)

    def columns(b, to_x, to_s):
        return pl.ds(pl.multiple_of(((b * 2 + to_x) * 2 + to_s) * half, half), half)

    def rows_of(m):
        return pl.ds(pl.multiple_of(m * tokens, tokens), tokens)

    def dot(a, b, ca, cb):
        return lax.dot_general(a, b, (((ca,), (cb,)), ((), ())), preferred_element_type=jnp.float32)

    def w_copy(c, k, upward):
        src_block = z - k if upward else z + k
        src = w_ref.at[c] if k == 0 else wb.at[c, block(src_block)]
        return remote(
            src, wb.at[c, block(src_block)],
            w_send.at[int(upward), c, k], w_recv.at[c, src_block], up if upward else down,
        )

    def w_arrival(c, k, upward):
        src_block = z - k if upward else z + k
        part = wb.at[c, block(src_block)]
        return remote(part, part, w_send.at[int(upward), c, k], w_recv.at[c, src_block], down if upward else up)

    def w_keep(c):
        return pltpu.make_async_copy(w_ref.at[c], wb.at[c, block(z)], own_w.at[c])

    def weights_own(c):
        @pl.when(has_up)
        def _():
            w_copy(c, 0, True).start()

        @pl.when(has_down)
        def _():
            w_copy(c, 0, False).start()

        w_keep(c).start()

    def weights_forward(c, k):
        @pl.when(z - k >= 0)
        def _():
            w_arrival(c, k, True).wait_recv()
            if k < nz - 1:
                @pl.when(has_up)
                def _():
                    w_copy(c, k, True).start()

        @pl.when(z + k < nz)
        def _():
            w_arrival(c, k, False).wait_recv()
            if k < nz - 1:
                @pl.when(has_down)
                def _():
                    w_copy(c, k, False).start()

    def n_copy(p, j):
        to_x, to_s = plane_xs[p]
        return remote(
            n_ref.at[:, columns(j, to_x, to_s)], nb.at[mine, rows_of(mp), block(j)],
            n_send.at[p, j], n_recv.at[p, j], plane[p],
        )

    def n_keep(j):
        return pltpu.make_async_copy(
            n_ref.at[:, columns(j, x, seg)], nb.at[mine, rows_of(mp), block(j)], own_n.at[j]
        )

    def f_copy(p, j, o):
        if p == 3:
            return remote(
                n_ref.at[:, columns(j, x, seg)], nb.at[mine, rows_of(mp), block(j)],
                f_send.at[p, j, o], f_recv.at[p, j, o], m_peer[o],
            )
        from_x, from_s = plane_xs[p]
        part = nb.at[from_x * 2 + from_s, rows_of(mp), block(j)]
        return remote(part, part, f_send.at[p, j, o], f_recv.at[p, j, o], m_peer[o])

    def tokens_send(j):
        for p in (2, 0, 1):
            n_copy(p, j).start()
        n_keep(j).start()
        for o in range(others):
            f_copy(3, j, o).start()

    def tokens_forward(j):
        for p in range(3):
            n_copy(p, j).wait_recv()
            for o in range(others):
                f_copy(p, j, o).start()

    def tokens_wait():
        for j in range(nz):
            n_keep(j).wait()
            for p in range(4):
                for o in range(others):
                    f_copy(p, j, o).wait_recv()

    tile = min(rows, 512)

    def tiles(body):
        if rows == tile:
            body(pl.ds(0, tile))
        else:
            @pl.loop(0, rows // tile)
            def _(i):
                body(pl.ds(pl.multiple_of(i * tile, tile), tile))

    def sample(c, a, b):
        return a * 2 + b if first_axis(c) == 0 else b * 2 + a

    def coords(c):
        return (x, seg) if first_axis(c) == 0 else (seg, x)

    def peers(c):
        return (plane[0], plane[1]) if first_axis(c) == 0 else (plane[1], plane[0])

    def p_copy(c):
        return remote(ps.at[c], px.at[c], p_send.at[c], p_recv.at[c], peers(c)[0])

    def y_copy(c):
        return remote(ys.at[c], yb.at[c], y_send.at[c], y_recv.at[c], peers(c)[1])

    def partial_sums(c):
        if c == 0:
            tokens_wait()
        w_keep(c).wait()
        a, _ = coords(c)

        @pl.loop(0, 2)
        def _(b):
            q = sample(c, 1 - a, b)

            def body(part):
                ps[c, b, part, :] = dot(nb[q, part, :], wb[c], 1, 0).astype(jnp.bfloat16)

            tiles(body)

        p_copy(c).start()

        @pl.loop(0, 2)
        def _(b):
            q = sample(c, a, b)

            def body(part):
                keep[c, b, part, :] = dot(nb[q, part, :], wb[c], 1, 0)

            tiles(body)

    def second_sums(c):
        _, b = coords(c)
        p_copy(c).wait_recv()
        ys[c] = (keep[c, 1 - b] + px[c, 1 - b].astype(jnp.float32)).astype(jnp.bfloat16)
        y_copy(c).start()
        keep[c, b] = keep[c, b] + px[c, b].astype(jnp.float32)

    def g_copy(c, i):
        one, two = peers(c)
        a, b = coords(c)
        q = sample(c, a, 1 - b) if i == 2 else mine
        part = gb.at[c, q]
        return remote(part, part, g_send.at[c, i], g_recv.at[c, i], two if i == 0 else one)

    vis = vis_ref[...]
    visible = jnp.concatenate([vis] * ratio, axis=0) > 0.5

    def attend(c):
        _, b = coords(c)
        y_copy(c).wait_recv()
        pair = (keep[c, b] + yb[c].astype(jnp.float32)).astype(jnp.bfloat16)
        cols = slice(c * HD, (c + 1) * HD)
        keys = jnp.concatenate([pair[:, :HD], akv_ref[0, :, cols]], axis=0)
        values = jnp.concatenate([pair[:, HD:], akv_ref[1, :, cols]], axis=0)
        hs = [slice((c * ratio + r) * HD, (c * ratio + r + 1) * HD) for r in range(ratio)]
        query = jnp.concatenate([q_ref[:, h] for h in hs], axis=0)
        go = jnp.concatenate([go_ref[:, h] for h in hs], axis=0)
        masked = jnp.where(visible, dot(query, keys, 1, 1) * scale, NEGATIVE)
        top = jnp.max(masked, axis=-1, keepdims=True)
        expo = jnp.where(visible, jnp.exp(masked - top), 0.0)
        probs = expo * (1.0 / jnp.sum(expo, axis=-1, keepdims=True))
        low = probs.astype(jnp.bfloat16)
        d_probs = dot(go, values, 1, 1)
        delta = jnp.sum(probs * d_probs, axis=-1, keepdims=True)
        d_scores = (probs * (d_probs - delta)).astype(jnp.bfloat16)
        d_keys = dot(d_scores, query, 0, 0) * scale
        d_values = dot(low, go, 0, 0)
        gb[c, mine, :, :HD] = d_keys[:rows].astype(jnp.bfloat16)
        gb[c, mine, :, HD:] = d_values[:rows].astype(jnp.bfloat16)
        g_copy(c, 0).start()
        g_copy(c, 1).start()
        dakv_ref[0, :, cols] = d_keys[rows:]
        dakv_ref[1, :, cols] = d_values[rows:]
        out = dot(low, values, 1, 0).astype(jnp.bfloat16)
        d_query = dot(d_scores, keys, 1, 0) * scale
        for r, h in enumerate(hs):
            out_ref[:, h] = out[r * acts : (r + 1) * acts]
            dq_ref[:, h] = d_query[r * acts : (r + 1) * acts]

    def grads_forward(c):
        g_copy(c, 0).wait_recv()
        g_copy(c, 2).start()

    depth = min(nz * half, 512)

    def weight_terms(c):
        g_copy(c, 1).wait_recv()
        g_copy(c, 2).wait_recv()

        @pl.loop(0, nz * half // depth)
        def _(i):
            cols = pl.ds(pl.multiple_of(i * depth, depth), depth)
            total = dot(nb[0, :, cols], gb[c, 0], 0, 0)
            for q in range(1, samples):
                total = total + dot(nb[q, :, cols], gb[c, q], 0, 0)
            dw[c % 2, cols, :] = total

    def z_copy(c, off, upward):
        to = z + off if upward else z - off
        slot = nz if (not upward and off == 1) else to
        return remote(
            zs.at[c, to], zb.at[c, slot], z_send.at[c, to], z_recv.at[c, slot], up if upward else down
        )

    def z_arrival(c, slot, upward):
        part = zb.at[c, slot]
        return remote(part, part, z_send.at[c, z], z_recv.at[c, slot], down if upward else up)

    def chain(c, off):
        def step(to, upward):
            @pl.when(has_down if upward else has_up)
            def _():
                z_arrival(c, to, upward).wait_recv()

            zs[c, to] = (dw[c % 2, block(to), :] + zb[c, to].astype(jnp.float32)).astype(jnp.bfloat16)
            z_copy(c, off, upward).start()

        @pl.when(z + off < nz)
        def _():
            step(z + off, True)

        @pl.when(z - off >= 0)
        def _():
            step(z - off, False)

    def o_copy(c):
        return remote(o_ref.at[c, seg], o_ref.at[c, seg], o_send.at[c], o_recv.at[c], plane[1])

    def finish(c):
        @pl.when(has_down)
        def _():
            z_arrival(c, z, True).wait_recv()

        @pl.when(has_up)
        def _():
            z_arrival(c, nz, False).wait_recv()

        total = dw[c % 2, block(z), :] + zb[c, z].astype(jnp.float32) + zb[c, nz].astype(jnp.float32)
        o_ref[c, seg] = total.astype(jnp.bfloat16)
        o_copy(c).start()

    def clear():
        @pl.when(z == 0)
        def _():
            @pl.loop(0, chunks)
            def _(c):
                @pl.loop(0, nz)
                def _(b):
                    zb[c, b] = jnp.zeros(zb.shape[2:], zb.dtype)

        @pl.when(z == nz - 1)
        def _():
            @pl.loop(0, chunks)
            def _(c):
                @pl.loop(0, nz - 1)
                def _(b):
                    zb[c, b] = jnp.zeros(zb.shape[2:], zb.dtype)

                zb[c, nz] = jnp.zeros(zb.shape[2:], zb.dtype)

    bodies = dict(
        wo=weights_own, wf=weights_forward, ns=tokens_send, nf=tokens_forward,
        A=partial_sums, B=second_sums, C=attend, G=grads_forward, D=weight_terms, E=chain, F=finish,
    )
    cleared = False
    for stage in order:
        if stage[0] not in ("wo", "ns") and not cleared:
            clear()
            cleared = True
        bodies[stage[0]](*stage[1:])

    for c in range(chunks):
        o_copy(c).wait()
        p_copy(c).wait_send()
        y_copy(c).wait_send()
        for i in range(3):
            g_copy(c, i).wait_send()
        for off in range(nz - 1, 0, -1):
            @pl.when(z + off < nz)
            def _():
                z_copy(c, off, True).wait_send()

            @pl.when(z - off >= 0)
            def _():
                z_copy(c, off, False).wait_send()

        for k in range(nz - 1):
            @pl.when(jnp.logical_and(has_up, z - k >= 0))
            def _():
                w_copy(c, k, True).wait_send()

            @pl.when(jnp.logical_and(has_down, z + k < nz))
            def _():
                w_copy(c, k, False).wait_send()

    for j in range(nz):
        for p in range(3):
            n_copy(p, j).wait_send()
        for p in range(4):
            for o in range(others):
                f_copy(p, j, o).wait_send()


def fused(nz, nmp, ratio, weight, normed, query, akv, grad_out, visible):
    dma = pltpu.SemaphoreType.DMA
    vmem = pl.BlockSpec(memory_space=pltpu.VMEM)
    chunks, half, _ = weight.shape
    tokens = normed.shape[0]
    rows = nmp * tokens
    deep = nz * half
    acts, width = query.shape
    others = max(nmp - 1, 1)
    bf16, f32 = jnp.bfloat16, jnp.float32
    order = stages(nz, chunks)
    return pl.pallas_call(
        functools.partial(kernel, order, nz, nmp, ratio),
        out_shape=(
            jax.ShapeDtypeStruct((acts, width), bf16),
            jax.ShapeDtypeStruct((acts, width), f32),
            jax.ShapeDtypeStruct(akv.shape, f32),
            jax.ShapeDtypeStruct((chunks, 2, half, PAIR), bf16),
        ),
        in_specs=[vmem] * 6,
        out_specs=(vmem,) * 4,
        scratch_shapes=[
            pltpu.VMEM((4, rows, deep), bf16),
            pltpu.VMEM((chunks, deep, PAIR), bf16),
            pltpu.VMEM((chunks, 2, rows, PAIR), f32),
            pltpu.VMEM((chunks, 2, rows, PAIR), bf16),
            pltpu.VMEM((chunks, 2, rows, PAIR), bf16),
            pltpu.VMEM((chunks, rows, PAIR), bf16),
            pltpu.VMEM((chunks, rows, PAIR), bf16),
            pltpu.VMEM((chunks, 4, rows, PAIR), bf16),
            pltpu.VMEM((2, deep, PAIR), f32),
            pltpu.VMEM((chunks, nz, half, PAIR), bf16),
            pltpu.VMEM((chunks, nz + 1, half, PAIR), bf16),
            dma((2, chunks, nz)), dma((chunks, nz)), dma((nz,)), dma((chunks,)),
            dma((3, nz)), dma((3, nz)), dma((4, nz, others)), dma((4, nz, others)),
            dma((chunks,)), dma((chunks,)), dma((chunks,)), dma((chunks,)),
            dma((chunks, 3)), dma((chunks, 3)),
            dma((chunks, nz)), dma((chunks, nz + 1)),
            dma((chunks,)), dma((chunks,)),
        ],
        compiler_params=pltpu.CompilerParams(
            collective_id=0, has_side_effects=True, vmem_limit_bytes=60 * MiB
        ),
        name="fused",
    )(weight, normed, query, akv, grad_out, visible)


def shards(
    ndp,
    nmp,
    prefix_hidden,
    norm_gain,
    kv_weight,
    action_query,
    action_kv,
    out_cotangent,
    prefix_blocks,
    action_blocks,
    prefix_lengths,
    timesteps,
):
    nz = ndp // 2
    ratio = QH // KVH
    depth, _, columns = kv_weight.shape
    chunks = columns // HD
    half = depth // 2
    seg = lax.axis_index("segment")
    wide = prefix_hidden[0].astype(jnp.float32)
    inverse = lax.rsqrt(jnp.mean(wide * wide, axis=-1, keepdims=True) + EPS)
    normed_local = (wide * inverse * norm_gain).astype(jnp.bfloat16)
    own_weight = lax.dynamic_slice_in_dim(kv_weight, seg * half, half, axis=0)
    own_weight = own_weight.reshape(half, 2, chunks, HD).transpose(2, 0, 1, 3).reshape(chunks, half, PAIR)
    rows = nmp * normed_local.shape[0]
    flow_weight = 0.5 + (timesteps[0].astype(jnp.float32) + 0.5) / STEPS
    grad_out = (flow_weight * out_cotangent[0].astype(jnp.float32)).astype(jnp.bfloat16)
    pblocks = prefix_blocks[0]
    ablocks = action_blocks[0]
    positions = jnp.arange(rows, dtype=jnp.int32)
    see_prefix = (pblocks[None, :] <= ablocks[:, None]) & (positions[None, :] < prefix_lengths[0])
    see_action = ablocks[None, :] <= ablocks[:, None]
    visible = jnp.concatenate([see_prefix, see_action], axis=1).astype(jnp.float32)
    attn_out, query_grad, d_action, summed = fused(
        nz, nmp, ratio, own_weight, normed_local,
        action_query[0], action_kv[0].transpose(1, 0, 2), grad_out, visible,
    )
    weight_grad = summed.reshape(chunks, depth, 2, HD).transpose(1, 2, 0, 3).reshape(depth, 2, columns)
    return (
        attn_out[None],
        query_grad[None],
        d_action.transpose(1, 0, 2)[None],
        weight_grad.astype(jnp.float32),
    )


def solution(mesh):
    placed = (
        P(("dp", "segment"), "mp", None),
        P(),
        P("dp", None, "mp"),
        P(("dp", "segment"), None, "mp"),
        P(("dp", "segment"), None, None, "mp"),
        P(("dp", "segment"), None, "mp"),
        P(("dp", "segment"), None),
        P(("dp", "segment"), None),
        P(("dp", "segment")),
        P(("dp", "segment")),
    )
    return jax.shard_map(
        functools.partial(shards, mesh.shape["dp"], mesh.shape["mp"]),
        mesh=mesh,
        in_specs=placed,
        out_specs=(
            P(("dp", "segment"), None, "mp"),
            P(("dp", "segment"), None, "mp"),
            P(("dp", "segment"), None, None, "mp"),
            P("dp", None, "mp"),
        ),
        check_vma=False,
    )
```

time: 258 us -> 229 us (0.89)
  Pallas kernels: 241 us -> 194 us
  local copies, waits for them, and re-layouts: 12 us -> 22.5 us
  other arithmetic: 2.98 us -> 10.2 us
    pallas_call x3 -> x1, Pallas kernels: 241 us -> 194 us  [fused(): pl.pallas_call(functools.partial(kernel, order, nz, nmp, ratio), out_shap...]
    convert_element_type x0 -> x2, local copies, waits for them, and re-layouts: none -> 10.8 us  [shards(): weight_grad.astype(jnp.float32)]
    convert_element_type x1, other arithmetic: 1.19 us -> 5.37 us  [shards(): normed_local = (wide * inverse * norm_gain).astype(jnp.bfloat16)]
    unnamed x22 -> x21, local copies, waits for them, and re-layouts: 9.89 us -> 6.98 us
where the time goes in v1:
time: 229 us
  Pallas kernels  194 us (85%)
  local copies, waits for them, and re-layouts  22.5 us (10%)
  other arithmetic  10.2 us (4%)
    pallas_call x1, Pallas kernels, fused(): pl.pallas_call(functools.partial(kernel, order, nz, nmp, ratio), out_shap...  194 us
    convert_element_type x2, local copies, waits for them, and re-layouts, shards(): weight_grad.astype(jnp.float32)  10.8 us
    unnamed x21, local copies, waits for them, and re-layouts  6.98 us
    convert_element_type x1, other arithmetic, shards(): normed_local = (wide * inverse * norm_gain).astype(jnp.bfloat16)  5.37 us

profile of v1, /device:TPU:0, one launch (start us, length us, event | category | flops | bytes accessed | tf_op | source)
XLA Modules:
  0.0 229.1 jit_solution(16840773248205867732)
XLA Ops:
  0.6 0.0 copy-start
  0.6 0.0 copy-start.6
  0.7 0.0 copy-start.7
  0.7 0.0 copy-start.2
  0.7 0.0 copy-start.3
  2.2 3.1 %fusion = f32[256]{0:T(256)S(1)} fusion(bf16[1,256,8192]{2,1,0:T(8,128)(2,1)} %param.10), kind=kLoop, calls=%fused_computation.2 | loop fusion | flops 6291200 | bytes 4195328 | tf_op jit(solution)/shard_map/reduce_sum | solution.py:544
  5.3 0.0 copy-done.6
  5.3 0.1 broadcast_compare_fusion
  5.4 0.0 copy-done.7
  5.4 0.1 compare_and_fusion
  5.5 0.8 add_convert_fusion.vis_ref
  6.2 0.0 copy-done.2
  6.2 0.8 fusion.3.go_ref
  7.0 0.0 copy-done.3
  7.0 0.7 copy.26
  7.7 0.0 copy-done
  7.7 0.0 copy-start.5
  7.7 0.7 constant_dynamic-slice_fusion
  8.5 2.5 %copy.22 = bf16[512,2,512]{0,2,1:T(8,128)(2,1)} copy(bf16[512,2,512]{2,1,0:T(2,128)(2,1)S(1)} %constant_dynamic-slice_fusion) | data formatting | bytes 2097152
  10.9 2.5 %copy.18 = bf16[4,512,2,128]{3,2,1,0:T(2,128)(2,1)S(1)} copy(bf16[4,512,2,128]{1,3,0,2:T(8,128)(2,1)} %bitcast.33) | data formatting | bytes 2097152 | tf_op jit(solution)/shard_map/transpose | solution.py:547
  13.4 1.5 reshape.49.w_ref
  14.9 0.0 copy-done.5
  14.9 5.4 %fusion.2.n_ref = bf16[256,8192]{1,0:T(8,128)(2,1)} fusion(bf16[1,256,8192]{2,1,0:T(8,128)(2,1)} %param.10, f32[8192]{0:T(1024)S(1)} %copy-done.5, f32[256]{0:T(256)S(1)} %add_rsqrt_fusion), kind=kLoop, calls=%fused_computation.4 | loop fusion | flops 8388608 | bytes 8422400 | tf_op jit(solution)/shard_map/convert_element_type | solution.py:545
  20.3 194.2 %fused.1 = (bf16[128,1024]{1,0:T(8,128)(2,1)}, f32[128,1024]{1,0:T(8,128)}, f32[2,128,512]{2,1,0:T(8,128)}, bf16[4,2,512,256]{3,2,1,0:T(8,128)(2,1)}) custom-call(bf16[4,512,256]{2,1,0:T(8,128)(2,1)} %reshape.49.w_ref, bf16[256,8192]{1,0:T(8,128)(2,1)} %fusion.2.n_ref, bf16[128,1024]{1,0:T(8,128)(2,1)} %bitcast.37, bf16[2,128,512]{2,1,0:T(8,128)(2,1)} %bitcast.34, ...), custom_call_target="tpu_custom_call" | custom-call | tf_op jit(solution)/shard_map/fused/pallas_call | solution.py:487
  214.5 2.2 copy.21
  216.8 5.1 %reshape.52 = f32[4,1024,2,128]{3,2,1,0:T(2,128)} reshape(bf16[4,2,512,256]{3,2,1,0:T(8,128)(2,1)} %get-tuple-element.11) | data formatting | bytes 6291456 | tf_op jit(solution)/shard_map/convert_element_type | solution.py:566
  221.9 0.0 copy-start.4
  221.9 0.0 copy-start.1
  221.9 5.7 %copy_bitcast_fusion = f32[1024,2,512]{2,1,0:T(2,128)} fusion(f32[4,1024,2,128]{3,2,1,0:T(2,128)} %reshape.52), kind=kLoop, calls=%fused_computation.5 | loop fusion | bytes 8388608 | tf_op jit(solution)/shard_map/convert_element_type | solution.py:566
  227.6 0.0 copy-done.4
  227.6 0.7 copy.31
  228.3 0.0 copy-done.1
  228.3 0.8 copy.32
  (2 shorter events, 0.0 us)
Async XLA Ops:
  0.6 7.1 %copy-start = (bf16[1024,2,512]{2,1,0:T(2,128)(2,1)S(1)}, bf16[1024,2,512]{2,1,0:T(2,128)(2,1)}, u32[]{:S(2)}) copy-start(bf16[1024,2,512]{2,1,0:T(2,128)(2,1)} %param.12) | copy-start | bytes 6291460
  0.6 4.6 %copy-start.6 = (s32[1,128]{1,0:T(1,128)S(1)}, s32[1,128]{1,0:T(1,128)}, u32[]{:S(2)}) copy-start(s32[1,128]{1,0:T(1,128)} %param.17) | copy-start | bytes 1540
  0.7 4.7 %copy-start.7 = (s32[1,512]{1,0:T(1,128)S(1)}, s32[1,512]{1,0:T(1,128)}, u32[]{:S(2)}) copy-start(s32[1,512]{1,0:T(1,128)} %param.16) | copy-start | bytes 6148
  0.7 5.6 %copy-start.2 = (bf16[1,128,1024]{2,1,0:T(8,128)(2,1)S(1)}, bf16[1,128,1024]{2,1,0:T(8,128)(2,1)}, u32[]{:S(2)}) copy-start(bf16[1,128,1024]{2,1,0:T(8,128)(2,1)} %param.15) | copy-start | bytes 786436
  0.7 6.3 %copy-start.3 = (bf16[1,128,2,512]{3,2,1,0:T(2,128)(2,1)S(1)}, bf16[1,128,2,512]{3,2,1,0:T(2,128)(2,1)}, u32[]{:S(2)}) copy-start(bf16[1,128,2,512]{3,2,1,0:T(2,128)(2,1)} %param.14) | copy-start | bytes 786436
  7.7 7.2 %copy-start.5 = (f32[8192]{0:T(1024)S(1)}, f32[8192]{0:T(1024)}, u32[]{:S(2)}) copy-start(f32[8192]{0:T(1024)} %param.11) | copy-start | bytes 98308
  221.9 5.7 %copy-start.4 = (bf16[128,1024]{1,0:T(8,128)(2,1)S(1)}, bf16[128,1024]{1,0:T(8,128)(2,1)}, u32[]{:S(2)}) copy-start(bf16[128,1024]{1,0:T(8,128)(2,1)} %get-tuple-element.8) | copy-start | bytes 786436
  221.9 6.4 %copy-start.1 = (f32[128,1024]{1,0:T(8,128)S(1)}, f32[128,1024]{1,0:T(8,128)}, u32[]{:S(2)}) copy-start(f32[128,1024]{1,0:T(8,128)} %get-tuple-element.9) | copy-start | bytes 1572868

commit v2 on v1

v2 whole, which is shorter than its diff:
```python
import functools

import jax
import jax.numpy as jnp
from jax import lax
from jax.experimental import pallas as pl
from jax.experimental.pallas import tpu as pltpu
from jax.sharding import PartitionSpec as P

HD = 128
QH = 16
KVH = 8
STEPS = 1000
EPS = 1e-06
NEGATIVE = -1e30
MiB = 1 << 20
PAIR = 2 * HD
KEPT = 3
STRIPS = 4
LIMIT = 45.5


def remote(src, dst, send_sem, recv_sem, where):
    return pltpu.make_async_remote_copy(
        src_ref=src,
        dst_ref=dst,
        send_sem=send_sem,
        recv_sem=recv_sem,
        device_id=where,
        device_id_type=pl.DeviceIdType.MESH,
    )


class Plan:
    def __init__(self, nz, chunks):
        self.nz, self.chunks = nz, chunks
        self.free = dict(core=0.0, x=0.0, s=0.0, z=0.0, m=0.0)
        self.arrived = {}
        self.pending = []
        self.order = []

    def add(self, key, needs, cost, sends, rank):
        self.pending.append((key, needs, cost, sends, rank))

    def run(self):
        done = set()
        while self.pending:
            best = None
            for entry in self.pending:
                key, needs, cost, sends, rank = entry
                if any(n not in self.arrived for n in needs):
                    continue
                ready = max([self.free["core"]] + [self.arrived[n] for n in needs])
                pick = (ready, rank)
                if best is None or pick < best[0]:
                    best = (pick, entry)
            (ready, _), entry = best
            self.pending.remove(entry)
            key, needs, cost, sends, rank = entry
            self.order.append(key)
            self.arrived[key] = ready + cost
            self.free["core"] = ready + cost
            for name, link, size in sends:
                start = max(ready + cost, self.free[link])
                self.free[link] = start + size
                self.arrived[name] = start + size + HOP
        return self.order


UNIT = 5.7
HOP = 1.7


FOUND = (
    ("ns", 0), ("ns", 1), ("wo", 0), ("ns", 2), ("wo", 1), ("wf", 0, 1), ("wf", 1, 1), ("wo", 2),
    ("wo", 3), ("ns", 3), ("wf", 2, 1), ("nf", 0), ("nf", 1), ("wf", 0, 2), ("nf", 2), ("wf", 1, 2),
    ("wf", 2, 2), ("nf", 3), ("wf", 0, 3), ("A", 0), ("B", 0, 1), ("wf", 1, 3), ("wf", 3, 1), ("B", 0, 0),
    ("A", 1), ("C", 0), ("wf", 2, 3), ("G", 0, 0), ("G", 0, 1), ("B", 1, 1), ("B", 1, 0), ("wf", 3, 2),
    ("A", 2), ("E", 0, 3), ("C", 1), ("E", 0, 2), ("G", 1, 1), ("E", 0, 1), ("G", 1, 0), ("B", 2, 1),
    ("wf", 3, 3), ("B", 2, 0), ("A", 3), ("E", 1, 3), ("E", 1, 2), ("C", 2), ("E", 1, 1), ("G", 2, 1),
    ("G", 2, 0), ("B", 3, 0), ("F", 0), ("B", 3, 1), ("E", 2, 3), ("E", 2, 2), ("C", 3), ("H", 0),
    ("E", 2, 1), ("G", 3, 0), ("G", 3, 1), ("F", 1), ("E", 3, 3), ("F", 2), ("E", 3, 2), ("H", 1),
    ("E", 3, 1), ("H", 2), ("F", 3), ("H", 3),
)


def stages(nz, chunks):
    made = modelled(nz, chunks)
    return list(FOUND) if set(FOUND) == set(made) else made


def modelled(nz, chunks):
    plan = Plan(nz, chunks)
    piece = UNIT
    for c in range(chunks):
        needs = [] if c < 2 else [("wf", c - 2, nz - 1)]
        plan.add(("wo", c), needs, 0.1, [(("w", c, 1), "z", piece)], c * 0.01)
        for k in range(1, nz):
            needs = [("w", c, k)] + ([("wf", c, k - 1)] if k > 1 else [("wo", c)])
            sends = [(("w", c, k + 1), "z", piece)] if k < nz - 1 else []
            plan.add(("wf", c, k), needs, 0.1, sends, 1)
    for j in range(STRIPS):
        needs = [("ns", j - 1)] if j else [("wo", 0)]
        plan.add(
            ("ns", j), needs, 0.1,
            [(("nx", j), "x", piece), (("ny", j), "s", piece), (("nd", j), "x", piece), (("nd2", j), "s", piece)], 0.005,
        )
        plan.add(("nf", j), [("nx", j), ("ny", j), ("nd", j), ("nd2", j)], 0.1, [(("nm", j), "m", 2.0)], 2)
    for c in range(chunks):
        needs = [("nm", j) for j in range(STRIPS)] + [("wf", c, k) for k in range(1, nz)]
        if c >= KEPT:
            needs.append(("C", c - KEPT))
        plan.add(("A", c), needs, 3.0, [(("p0", c), "x", piece), (("p1", c), "s", piece)], 10 + c)
        plan.add(("B", c, 0), [("A", c), ("p0", c)], 0.3, [(("y0", c), "s", piece / 2)], 7)
        plan.add(("B", c, 1), [("A", c), ("p1", c)], 0.3, [(("y1", c), "x", piece / 2)], 7)
        plan.add(
            ("C", c), [("B", c, 0), ("B", c, 1), ("y0", c), ("y1", c)], 2.5,
            [
                (("gx1", c), "x", piece / 2), (("gs0", c), "s", piece / 2),
                (("gx0", c), "x", piece / 2), (("gs1", c), "s", piece / 2),
            ], 6,
        )
        plan.add(("G", c, 0), [("C", c), ("gs0", c)], 0.1, [(("gf0", c), "x", piece / 2)], 4)
        plan.add(("G", c, 1), [("C", c), ("gx1", c)], 0.1, [(("gf1", c), "s", piece / 2)], 4)
        full = [("G", c, 0), ("G", c, 1), ("gx0", c), ("gs1", c), ("gf0", c), ("gf1", c)]
        for off in range(nz - 1, 0, -1):
            needs = full if off == nz - 1 else [("E", c, off + 1), ("e", c, off + 1)]
            plan.add(("E", c, off), needs, 1.2, [(("e", c, off), "z", piece)], 3)
        plan.add(("F", c), [("E", c, 1), ("e", c, 1)], 1.3, [(("o", c), "s", piece)], 5)
        plan.add(("H", c), [("F", c), ("o", c)], 0.5, [], 20)
    return plan.run()


def kernel(
    order, nz, nmp, ratio,
    w_hbm, h_hbm, gain_hbm, level_ref, length_ref, q_hbm, akv_hbm, cot_hbm, pb_hbm, ab_hbm,
    out_ref, dq_ref, dakv_ref, grad_ref,
    gain_ref, vis_ref, q_ref, akv_ref, cot_ref, pb_ref, ab_ref, w_raw, h_buf, n_ref, o_ref, nb, wb, keep, ps, px, ys, yb, gb, zs, zb,
    w_send, w_recv, own_n, load_w, load_h, load_more, n_send, n_recv, f_send, f_recv,
    p_send, p_recv, y_send, y_recv, g_send, g_recv, z_send, z_recv, o_send, o_recv,
):
    dp, seg, mp = lax.axis_index("dp"), lax.axis_index("segment"), lax.axis_index("mp")
    z, x = dp // 2, dp % 2
    chunks, half = wb.shape[0], w_raw.shape[0]
    tokens, features = h_hbm.shape
    strip = tokens // STRIPS
    samples, rows = nb.shape[0], nb.shape[1]
    others = nmp - 1
    acts = q_ref.shape[0]
    scale = HD ** (-0.5)

    x_dp = z * 2 + (1 - x)
    plane = [
        {"dp": x_dp},
        {"segment": 1 - seg},
        {"dp": x_dp, "segment": 1 - seg},
    ]
    plane_xs = [(1 - x, seg), (x, 1 - seg), (1 - x, 1 - seg)]
    m_peer = [{"mp": (mp + o) % nmp} for o in range(1, nmp)]
    up = {"dp": (z + 1) * 2 + x}
    down = {"dp": (z - 1) * 2 + x}
    has_up, has_down = z < nz - 1, z > 0
    mine = x * 2 + seg

    def h_load(j):
        return pltpu.make_async_copy(h_hbm.at[pl.ds(j * strip, strip)], h_buf.at[j % 2], load_h.at[j % 2])

    w_load = pltpu.make_async_copy(w_hbm.at[pl.ds(pl.multiple_of(seg * half, half), half)], w_raw, load_w.at[0])
    more = [
        pltpu.make_async_copy(src, dst, load_more.at[i])
        for i, (src, dst) in enumerate(
            [(gain_hbm, gain_ref), (q_hbm, q_ref), (akv_hbm, akv_ref), (cot_hbm, cot_ref), (pb_hbm, pb_ref), (ab_hbm, ab_ref)]
        )
    ]
    h_load(0).start()
    more[0].start()
    w_load.start()
    h_load(1).start()
    for copy in more[1:]:
        copy.start()

    barrier = pltpu.get_barrier_semaphore()
    for peer in plane + m_peer:
        pl.semaphore_signal(barrier, inc=1, device_id=peer, device_id_type=pl.DeviceIdType.MESH)

    @pl.when(has_up)
    def _():
        pl.semaphore_signal(barrier, inc=1, device_id=up, device_id_type=pl.DeviceIdType.MESH)

    @pl.when(has_down)
    def _():
        pl.semaphore_signal(barrier, inc=1, device_id=down, device_id_type=pl.DeviceIdType.MESH)

    ends = has_up.astype(jnp.int32) + has_down.astype(jnp.int32)
    pl.semaphore_wait(barrier, len(plane) + len(m_peer) + ends)

    def block(b):
        return pl.ds(pl.multiple_of(b * half, half), half)

    def rows_of(m, j):
        return pl.ds(pl.multiple_of(m * tokens + j * strip, strip), strip)

    def dot(a, b, ca, cb):
        return lax.dot_general(a, b, (((ca,), (cb,)), ((), ())), preferred_element_type=jnp.float32)

    def w_copy(c, k, upward):
        src_block = z - k if upward else z + k
        part = wb.at[c, block(src_block)]
        return remote(
            part, part,
            w_send.at[int(upward), c, k], w_recv.at[c, src_block], up if upward else down,
        )

    def w_arrival(c, k, upward):
        src_block = z - k if upward else z + k
        part = wb.at[c, block(src_block)]
        return remote(part, part, w_send.at[int(upward), c, k], w_recv.at[c, src_block], down if upward else up)

    def weights_own(c):
        if c == 0:
            w_load.wait()
        group = min(half, 128)

        @pl.loop(0, half // group)
        def _(i):
            first = pl.multiple_of(i * group, group)
            for kv in range(2):
                wb[c, pl.ds(pl.multiple_of(z * half + first, group), group), kv * HD : (kv + 1) * HD] = w_raw[
                    pl.ds(first, group), kv, c * HD : (c + 1) * HD
                ]

        @pl.when(has_up)
        def _():
            w_copy(c, 0, True).start()

        @pl.when(has_down)
        def _():
            w_copy(c, 0, False).start()

    def weights_forward(c, k):
        @pl.when(z - k >= 0)
        def _():
            w_arrival(c, k, True).wait_recv()
            if k < nz - 1:
                @pl.when(has_up)
                def _():
                    w_copy(c, k, True).start()

        @pl.when(z + k < nz)
        def _():
            w_arrival(c, k, False).wait_recv()
            if k < nz - 1:
                @pl.when(has_down)
                def _():
                    w_copy(c, k, False).start()

    plane_q = [a * 2 + b for a, b in plane_xs]

    def n_copy(p, j):
        return remote(
            n_ref.at[plane_q[p], pl.ds(j * strip, strip)], nb.at[mine, rows_of(mp, j)],
            n_send.at[p, j], n_recv.at[p, j], plane[p],
        )

    def n_keep(j):
        return pltpu.make_async_copy(
            n_ref.at[mine, pl.ds(j * strip, strip)], nb.at[mine, rows_of(mp, j)], own_n.at[j]
        )

    def f_copy(p, j, o):
        if p == 3:
            return remote(
                n_ref.at[mine, pl.ds(j * strip, strip)], nb.at[mine, rows_of(mp, j)],
                f_send.at[p, j, o], f_recv.at[p, j, o], m_peer[o],
            )
        part = nb.at[plane_q[p], rows_of(mp, j)]
        return remote(part, part, f_send.at[p, j, o], f_recv.at[p, j, o], m_peer[o])

    def normalize(j):
        h_load(j).wait()
        if j == 0:
            more[0].wait()
        group = min(strip, 16)
        wide = 1024 if features % 1024 == 0 else half

        @pl.loop(0, strip // group)
        def _(i):
            part = pl.ds(pl.multiple_of(i * group, group), group)
            into = pl.ds(pl.multiple_of(j * strip + i * group, group), group)
            total = jnp.zeros((group, 1), jnp.float32)
            for k in range(0, features, wide):
                piece = h_buf[j % 2, part, k : k + wide].astype(jnp.float32)
                total = total + jnp.sum(piece * piece, axis=-1, keepdims=True)
            inverse = lax.rsqrt(total / features + EPS)
            for b in range(nz):
                for q in range(4):
                    first = (b * 4 + q) * half
                    piece = h_buf[j % 2, part, first : first + half].astype(jnp.float32)
                    scaled = piece * inverse * gain_ref[:, first : first + half]
                    n_ref[q, into, b * half : (b + 1) * half] = scaled.astype(jnp.bfloat16)

        if j + 2 < STRIPS:
            h_load(j + 2).start()

    def tokens_send(j):
        normalize(j)
        for p in (2, 0, 1):
            n_copy(p, j).start()
        n_keep(j).start()
        for o in range(others):
            f_copy(3, j, o).start()

    def tokens_forward(j):
        for p in range(3):
            n_copy(p, j).wait_recv()
            for o in range(others):
                f_copy(p, j, o).start()

    def tokens_wait():
        for j in range(STRIPS):
            n_keep(j).wait()
            for p in range(4):
                for o in range(others):
                    f_copy(p, j, o).wait_recv()

    part_rows = rows // 2
    halves = [pl.ds(0, part_rows), pl.ds(part_rows, part_rows)]
    spot = [seg, x]

    def sample(h, first, second):
        return first * 2 + second if h == 0 else second * 2 + first

    def p_copy(c, h, i):
        b = spot[h] if i else 1 - spot[h]
        return remote(ps.at[c, h, b], px.at[c, h, b], p_send.at[c, h, i], p_recv.at[c, h, i], plane[h])

    def y_copy(c, h):
        return remote(ys.at[c, h], yb.at[c, h], y_send.at[c, h], y_recv.at[c, h], plane[1 - h])

    def partial_sums(c):
        if c == 0:
            tokens_wait()
        for i in range(2):
            for h in range(2):
                b = spot[h] if i else 1 - spot[h]
                q = sample(h, 1 - (x, seg)[h], b)
                ps[c, h, b] = dot(nb[q, halves[h], :], wb[c], 1, 0).astype(jnp.bfloat16)
                p_copy(c, h, i).start()
        for h in range(2):
            @pl.loop(0, 2)
            def _(b):
                q = sample(h, (x, seg)[h], b)
                keep[c % KEPT, h, b] = dot(nb[q, halves[h], :], wb[c], 1, 0)

    def second_sums(c, h):
        b = spot[h]
        p_copy(c, h, 0).wait_recv()
        ys[c, h] = (keep[c % KEPT, h, 1 - b] + px[c, h, 1 - b].astype(jnp.float32)).astype(jnp.bfloat16)
        y_copy(c, h).start()

    def g_copy(c, to, h):
        part = gb.at[c, mine, halves[h]]
        return remote(part, part, g_send.at[c, to, h], g_recv.at[c, to, h], plane[to])

    def g_forward(c, h):
        q = sample(h, (x, seg)[h], 1 - spot[h])
        part = gb.at[c, q, halves[h]]
        return remote(part, part, g_send.at[c, 2, h], g_recv.at[c, 2, h], plane[h])

    def visible_tokens():
        wide = jnp.broadcast_to(ab_ref[...].astype(jnp.float32), (acts, acts))
        levels = wide.T
        see_action = wide <= levels
        levels = jnp.concatenate([levels] * (rows // acts), axis=1)
        place = lax.broadcasted_iota(jnp.int32, (acts, rows), 1)
        see_prefix = (pb_ref[...].astype(jnp.float32) <= levels) & (place < length_ref[0])
        return jnp.concatenate([see_prefix.astype(jnp.float32), see_action.astype(jnp.float32)], axis=1)

    def attend(c):
        if c == 0:
            for copy in more[1:]:
                copy.wait()
            vis_ref[...] = visible_tokens()
        visible = jnp.concatenate([vis_ref[...]] * ratio, axis=0) > 0.5
        parts = []
        for h in range(2):
            y_copy(c, h).wait_recv()
            p_copy(c, h, 1).wait_recv()
            b = spot[h]
            parts.append(
                keep[c % KEPT, h, b] + px[c, h, b].astype(jnp.float32) + yb[c, h].astype(jnp.float32)
            )
        pair = jnp.concatenate(parts, axis=0).astype(jnp.bfloat16)
        cols = slice(c * HD, (c + 1) * HD)
        keys = jnp.concatenate([pair[:, :HD], akv_ref[:, 0, cols]], axis=0)
        values = jnp.concatenate([pair[:, HD:], akv_ref[:, 1, cols]], axis=0)
        hs = [slice((c * ratio + r) * HD, (c * ratio + r + 1) * HD) for r in range(ratio)]
        query = jnp.concatenate([q_ref[:, h] for h in hs], axis=0)
        cot = jnp.concatenate([cot_ref[:, h] for h in hs], axis=0)
        go = (level_ref[0] * cot.astype(jnp.float32)).astype(jnp.bfloat16)
        masked = jnp.where(visible, dot(query, keys, 1, 1) * scale, NEGATIVE)
        top = jnp.max(masked, axis=-1, keepdims=True)
        expo = jnp.where(visible, jnp.exp(masked - top), 0.0)
        probs = expo * (1.0 / jnp.sum(expo, axis=-1, keepdims=True))
        low = probs.astype(jnp.bfloat16)
        d_probs = dot(go, values, 1, 1)
        delta = jnp.sum(probs * d_probs, axis=-1, keepdims=True)
        d_scores = (probs * (d_probs - delta)).astype(jnp.bfloat16)
        d_keys = dot(d_scores, query, 0, 0) * scale
        d_values = dot(low, go, 0, 0)
        gb[c, mine, :, :HD] = d_keys[:rows].astype(jnp.bfloat16)
        gb[c, mine, :, HD:] = d_values[:rows].astype(jnp.bfloat16)
        for h in range(2):
            g_copy(c, 0, 1 - h).start()
            g_copy(c, 1, h).start()
        dakv_ref[:, 0, cols] = d_keys[rows:]
        dakv_ref[:, 1, cols] = d_values[rows:]
        out = dot(low, values, 1, 0).astype(jnp.bfloat16)
        d_query = dot(d_scores, keys, 1, 0) * scale
        for r, h in enumerate(hs):
            out_ref[:, h] = out[r * acts : (r + 1) * acts]
            dq_ref[:, h] = d_query[r * acts : (r + 1) * acts]

    def grads_forward(c, h):
        g_copy(c, 1 - h, h).wait_recv()
        g_forward(c, h).start()

    def grads_wait(c):
        for h in range(2):
            g_copy(c, h, h).wait_recv()
            g_forward(c, h).wait_recv()

    cuts = 2 if half % 256 == 0 else 1
    depth = half // cuts

    def weight_term(c, b, i):
        cols = pl.ds(pl.multiple_of(b * half + i * depth, depth), depth)
        total = dot(nb[0, :, cols], gb[c, 0], 0, 0)
        for q in range(1, samples):
            total = total + dot(nb[q, :, cols], gb[c, q], 0, 0)
        return total

    def half_of(i):
        return pl.ds(pl.multiple_of(i * depth, depth), depth)

    def z_copy(c, off, upward, i):
        to = z + off if upward else z - off
        slot = nz if (not upward and off == 1) else to
        return remote(
            zs.at[c, to, half_of(i)], zb.at[c, slot, half_of(i)],
            z_send.at[c, to, i], z_recv.at[c, slot, i], up if upward else down,
        )

    def z_arrival(c, slot, upward, i):
        part = zb.at[c, slot, half_of(i)]
        return remote(part, part, z_send.at[c, z, i], z_recv.at[c, slot, i], down if upward else up)

    def chain(c, off):
        if off == nz - 1:
            grads_wait(c)

        def step(to, upward):
            @pl.loop(0, cuts)
            def _(i):
                total = weight_term(c, to, i)

                @pl.when(has_down if upward else has_up)
                def _():
                    z_arrival(c, to, upward, i).wait_recv()

                zs[c, to, half_of(i), :] = (total + zb[c, to, half_of(i), :].astype(jnp.float32)).astype(jnp.bfloat16)
                z_copy(c, off, upward, i).start()

        @pl.when(z + off < nz)
        def _():
            step(z + off, True)

        @pl.when(z - off >= 0)
        def _():
            step(z - off, False)

    def o_copy(c, i):
        return remote(
            zs.at[c, z, half_of(i)], o_ref.at[c, half_of(i)], o_send.at[c, i], o_recv.at[c, i], plane[1]
        )

    def finish(c):
        @pl.loop(0, cuts)
        def _(i):
            part = half_of(i)
            total = weight_term(c, z, i)

            @pl.when(has_down)
            def _():
                z_arrival(c, z, True, i).wait_recv()

            @pl.when(has_up)
            def _():
                z_arrival(c, nz, False, i).wait_recv()

            total = total + zb[c, z, part, :].astype(jnp.float32) + zb[c, nz, part, :].astype(jnp.float32)
            zs[c, z, part, :] = total.astype(jnp.bfloat16)
            o_copy(c, i).start()

        spread(c, seg, zs.at[c, z])

    def spread(c, which, src):
        for i in range(2):
            first = which * (half * 2 * chunks) + c * 2 + i
            part = pl.ds(first, half, stride=2 * chunks)
            grad_ref[part, :] = src[:, i * HD : (i + 1) * HD].astype(jnp.float32)

    def other_half(c):
        for i in range(cuts):
            o_copy(c, i).wait()
        spread(c, 1 - seg, o_ref.at[c])

    def clear():
        @pl.when(z == 0)
        def _():
            @pl.loop(0, chunks)
            def _(c):
                @pl.loop(0, nz)
                def _(b):
                    zb[c, b] = jnp.zeros(zb.shape[2:], zb.dtype)

        @pl.when(z == nz - 1)
        def _():
            @pl.loop(0, chunks)
            def _(c):
                @pl.loop(0, nz - 1)
                def _(b):
                    zb[c, b] = jnp.zeros(zb.shape[2:], zb.dtype)

                zb[c, nz] = jnp.zeros(zb.shape[2:], zb.dtype)

    bodies = dict(
        wo=weights_own, wf=weights_forward, ns=tokens_send, nf=tokens_forward,
        A=partial_sums, B=second_sums, C=attend, G=grads_forward, E=chain, F=finish, H=other_half,
    )
    cleared = False
    for stage in order:
        if stage[0] not in ("wo", "ns") and not cleared:
            clear()
            cleared = True
        bodies[stage[0]](*stage[1:])

    for c in range(chunks):
        for h in range(2):
            p_copy(c, h, 0).wait_send()
            p_copy(c, h, 1).wait_send()
            y_copy(c, h).wait_send()
            for to in range(2):
                g_copy(c, to, h).wait_send()
            g_forward(c, h).wait_send()
        for off in range(nz - 1, 0, -1):
            @pl.when(z + off < nz)
            def _():
                for i in range(cuts):
                    z_copy(c, off, True, i).wait_send()

            @pl.when(z - off >= 0)
            def _():
                for i in range(cuts):
                    z_copy(c, off, False, i).wait_send()

        for k in range(nz - 1):
            @pl.when(jnp.logical_and(has_up, z - k >= 0))
            def _():
                w_copy(c, k, True).wait_send()

            @pl.when(jnp.logical_and(has_down, z + k < nz))
            def _():
                w_copy(c, k, False).wait_send()

    for j in range(STRIPS):
        for p in range(3):
            n_copy(p, j).wait_send()
        for p in range(4):
            for o in range(others):
                f_copy(p, j, o).wait_send()


def stay(array):
    return pltpu.with_memory_space_constraint(array, pltpu.HBM)


def fused(nz, nmp, ratio, weight, hidden, gain, level, length, query, akv, cotangent, pblocks, ablocks):
    dma = pltpu.SemaphoreType.DMA
    vmem = pl.BlockSpec(memory_space=pltpu.VMEM)
    smem = pl.BlockSpec(memory_space=pltpu.SMEM)
    anywhere = pl.BlockSpec(memory_space=pltpu.HBM)
    half, chunks = weight.shape[0] // 2, weight.shape[2] // HD
    tokens, features = hidden.shape
    rows = nmp * tokens
    deep = nz * half
    acts, width = query.shape
    others = max(nmp - 1, 1)
    bf16, f32 = jnp.bfloat16, jnp.float32
    order = stages(nz, chunks)
    return pl.pallas_call(
        functools.partial(kernel, order, nz, nmp, ratio),
        out_shape=(
            jax.ShapeDtypeStruct((acts, width), bf16),
            jax.ShapeDtypeStruct((acts, width), f32),
            jax.ShapeDtypeStruct(akv.shape, f32),
            jax.ShapeDtypeStruct((2 * half * chunks * 2, HD), f32),
        ),
        in_specs=[anywhere] * 3 + [smem] * 2 + [anywhere] * 5,
        out_specs=(vmem,) * 4,
        scratch_shapes=[
            pltpu.VMEM(gain.shape, f32),
            pltpu.VMEM((acts, rows + acts), f32),
            pltpu.VMEM(query.shape, bf16),
            pltpu.VMEM(akv.shape, bf16),
            pltpu.VMEM(cotangent.shape, bf16),
            pltpu.VMEM(pblocks.shape, jnp.int32),
            pltpu.VMEM(ablocks.shape, jnp.int32),
            pltpu.VMEM((half,) + weight.shape[1:], bf16),
            pltpu.VMEM((2, tokens // STRIPS, features), bf16),
            pltpu.VMEM((4, tokens, deep), bf16),
            pltpu.VMEM((chunks, half, PAIR), bf16),
            pltpu.VMEM((4, rows, deep), bf16),
            pltpu.VMEM((chunks, deep, PAIR), bf16),
            pltpu.VMEM((min(chunks, KEPT), 2, 2, rows // 2, PAIR), f32),
            pltpu.VMEM((chunks, 2, 2, rows // 2, PAIR), bf16),
            pltpu.VMEM((chunks, 2, 2, rows // 2, PAIR), bf16),
            pltpu.VMEM((chunks, 2, rows // 2, PAIR), bf16),
            pltpu.VMEM((chunks, 2, rows // 2, PAIR), bf16),
            pltpu.VMEM((chunks, 4, rows, PAIR), bf16),
            pltpu.VMEM((chunks, nz, half, PAIR), bf16),
            pltpu.VMEM((chunks, nz + 1, half, PAIR), bf16),
            dma((2, chunks, nz)), dma((chunks, nz)), dma((STRIPS,)), dma((1,)), dma((2,)), dma((6,)),
            dma((3, STRIPS)), dma((3, STRIPS)), dma((4, STRIPS, others)), dma((4, STRIPS, others)),
            dma((chunks, 2, 2)), dma((chunks, 2, 2)), dma((chunks, 2)), dma((chunks, 2)),
            dma((chunks, 3, 2)), dma((chunks, 3, 2)),
            dma((chunks, nz, 2)), dma((chunks, nz + 1, 2)),
            dma((chunks, 2)), dma((chunks, 2)),
        ],
        compiler_params=pltpu.CompilerParams(
            collective_id=0, has_side_effects=True, vmem_limit_bytes=int(LIMIT * MiB)
        ),
        name="fused",
    )(
        *[stay(a) for a in (weight, hidden, gain)],
        level,
        length,
        *[stay(a) for a in (query, akv, cotangent, pblocks, ablocks)],
    )


def shards(
    ndp,
    nmp,
    prefix_hidden,
    norm_gain,
    kv_weight,
    action_query,
    action_kv,
    out_cotangent,
    prefix_blocks,
    action_blocks,
    prefix_lengths,
    timesteps,
):
    nz = ndp // 2
    ratio = QH // KVH
    depth, _, columns = kv_weight.shape
    chunks = columns // HD
    level = 0.5 + (timesteps.astype(jnp.float32) + 0.5) / STEPS
    attn_out, query_grad, d_action, summed = fused(
        nz, nmp, ratio, kv_weight, prefix_hidden[0], norm_gain[None], level, prefix_lengths,
        action_query[0], action_kv[0], out_cotangent[0], prefix_blocks, action_blocks,
    )
    weight_grad = summed.reshape(depth, chunks, 2, HD).transpose(0, 2, 1, 3).reshape(depth, 2, columns)
    return (
        attn_out[None],
        query_grad[None],
        d_action[None],
        weight_grad,
    )


def solution(mesh):
    placed = (
        P(("dp", "segment"), "mp", None),
        P(),
        P("dp", None, "mp"),
        P(("dp", "segment"), None, "mp"),
        P(("dp", "segment"), None, None, "mp"),
        P(("dp", "segment"), None, "mp"),
        P(("dp", "segment"), None),
        P(("dp", "segment"), None),
        P(("dp", "segment")),
        P(("dp", "segment")),
    )
    return jax.shard_map(
        functools.partial(shards, mesh.shape["dp"], mesh.shape["mp"]),
        mesh=mesh,
        in_specs=placed,
        out_specs=(
            P(("dp", "segment"), None, "mp"),
            P(("dp", "segment"), None, "mp"),
            P(("dp", "segment"), None, None, "mp"),
            P("dp", None, "mp"),
        ),
        check_vma=False,
    )
```

time: 229 us -> 164 us (0.72)
  Pallas kernels: 194 us -> 158 us
  local copies, waits for them, and re-layouts: 22.5 us -> 4.3 us
  other arithmetic: 10.2 us -> 0 us
    pallas_call x1, Pallas kernels: 194 us -> 158 us  [fused(): pl.pallas_call(functools.partial(kernel, order, nz, nmp, ratio), out_shap...]
    convert_element_type x2 -> x0, local copies, waits for them, and re-layouts: 10.8 us -> none  [shards(): weight_grad.astype(jnp.float32)]
    convert_element_type x3 -> x0, other arithmetic: 6.88 us -> none  [the longest x1 5.37 us: shards(): normed_local = (wide * inverse * norm_gain).astype(jnp.bfloat16)]
    reduce_sum x1 -> x0, other arithmetic: 3.1 us -> none  [shards(): inverse = lax.rsqrt(jnp.mean(wide * wide, axis=-1, keepdims=True) + EPS)]
    unnamed x21 -> x4, local copies, waits for them, and re-layouts: 6.98 us -> 4.3 us
    transpose x1 -> x0, local copies, waits for them, and re-layouts: 2.45 us -> none  [shards(): own_weight.reshape(half, 2, chunks, HD).transpose(2, 0, 1, 3)]
where the time goes in v2:
time: 164 us
  Pallas kernels  158 us (96%)
  local copies, waits for them, and re-layouts  4.3 us (3%)
  between operations  1.94 us (1%)
    pallas_call x1, Pallas kernels, fused(): pl.pallas_call(functools.partial(kernel, order, nz, nmp, ratio), out_shap...  158 us
    unnamed x4, local copies, waits for them, and re-layouts  4.3 us

profile of v2, /device:TPU:0, one launch (start us, length us, event | category | flops | bytes accessed | tf_op | source)
XLA Modules:
  0.0 164.3 jit_solution(842048206747063970)
XLA Ops:
  1.9 158.1 %fused.1 = (bf16[128,1024]{1,0:T(8,128)(2,1)S(1)}, f32[128,1024]{1,0:T(8,128)S(1)}, f32[128,2,512]{2,1,0:T(2,128)S(1)}, f32[8192,128]{1,0:T(8,128)S(1)}) custom-call(bf16[1024,2,512]{2,1,0:T(2,128)(2,1)} %w_hbm.1, bf16[256,8192]{1,0:T(8,128)(2,1)} %bitcast.17, f32[1,8192]{1,0:T(1,128)} %bitcast.21, f32[1]{0:T(128)S(6)} %add.7.level_ref, ...), custom_call_target="tpu_custom_call" | custom-call | tf_op jit(solution)/shard_map/fused/pallas_call | solution.py:601
  160.0 0.7 copy.21
  160.7 0.8 copy.22
  161.5 0.8 copy.23
  162.3 2.0 %copy.24 = f32[1024,2,512]{2,1,0:T(2,128)} copy(f32[1024,2,512]{2,1,0:T(2,128)S(1)} %bitcast.13) | data formatting | bytes 8388608

commit v3 on v2

--- a/solution.py
+++ b/solution.py
@@ -16,7 +16,8 @@
 MiB = 1 << 20
 PAIR = 2 * HD
 KEPT = 3
-STRIPS = 4
+CUTS = 4
+STRIPS = 8
 LIMIT = 45.5
 
 
@@ -72,9 +73,10 @@
 
 
 FOUND = (
-    ("ns", 0), ("ns", 1), ("wo", 0), ("ns", 2), ("wo", 1), ("wf", 0, 1), ("wf", 1, 1), ("wo", 2),
-    ("wo", 3), ("ns", 3), ("wf", 2, 1), ("nf", 0), ("nf", 1), ("wf", 0, 2), ("nf", 2), ("wf", 1, 2),
-    ("wf", 2, 2), ("nf", 3), ("wf", 0, 3), ("A", 0), ("B", 0, 1), ("wf", 1, 3), ("wf", 3, 1), ("B", 0, 0),
+    ("ns", 0), ("wo", 0), ("ns", 1), ("ns", 2), ("ns", 3), ("ns", 4), ("ns", 5), ("wo", 1),
+    ("wf", 0, 1), ("wf", 1, 1), ("wo", 2), ("wo", 3), ("ns", 6), ("ns", 7), ("wf", 2, 1), ("nf", 0),
+    ("nf", 1), ("nf", 2), ("nf", 3), ("wf", 0, 2), ("nf", 4), ("nf", 5), ("wf", 1, 2), ("wf", 2, 2),
+    ("nf", 6), ("nf", 7), ("wf", 0, 3), ("A", 0), ("B", 0, 1), ("wf", 1, 3), ("wf", 3, 1), ("B", 0, 0),
     ("A", 1), ("C", 0), ("wf", 2, 3), ("G", 0, 0), ("G", 0, 1), ("B", 1, 1), ("B", 1, 0), ("wf", 3, 2),
     ("A", 2), ("E", 0, 3), ("C", 1), ("E", 0, 2), ("G", 1, 1), ("E", 0, 1), ("G", 1, 0), ("B", 2, 1),
     ("wf", 3, 3), ("B", 2, 0), ("A", 3), ("E", 1, 3), ("E", 1, 2), ("C", 2), ("E", 1, 1), ("G", 2, 1),
@@ -430,7 +432,7 @@
             g_copy(c, h, h).wait_recv()
             g_forward(c, h).wait_recv()
 
-    cuts = 2 if half % 256 == 0 else 1
+    cuts = next(n for n in (CUTS, 2, 1) if half % (n * 128) == 0)
     depth = half // cuts
 
     def weight_term(c, b, i):
@@ -634,8 +636,8 @@
             dma((3, STRIPS)), dma((3, STRIPS)), dma((4, STRIPS, others)), dma((4, STRIPS, others)),
             dma((chunks, 2, 2)), dma((chunks, 2, 2)), dma((chunks, 2)), dma((chunks, 2)),
             dma((chunks, 3, 2)), dma((chunks, 3, 2)),
-            dma((chunks, nz, 2)), dma((chunks, nz + 1, 2)),
-            dma((chunks, 2)), dma((chunks, 2)),
+            dma((chunks, nz, CUTS)), dma((chunks, nz + 1, CUTS)),
+            dma((chunks, CUTS)), dma((chunks, CUTS)),
         ],
         compiler_params=pltpu.CompilerParams(
             collective_id=0, has_side_effects=True, vmem_limit_bytes=int(LIMIT * MiB)
@@ -647,6 +649,30 @@
         length,
         *[stay(a) for a in (query, akv, cotangent, pblocks, ablocks)],
     )
+
+
+def settle_kernel(*refs):
+    count = (len(refs) - 1) // 2
+    copies = [
+        pltpu.make_async_copy(src, dst, refs[-1].at[i])
+        for i, (src, dst) in enumerate(zip(refs[:count], refs[count:-1]))
+    ]
+    for copy in copies:
+        copy.start()
+    for copy in copies:
+        copy.wait()
+
+
+def settle(*arrays):
+    return pl.pallas_call(
+        settle_kernel,
+        out_shape=tuple(jax.ShapeDtypeStruct(a.shape, a.dtype) for a in arrays),
+        in_specs=[pl.BlockSpec(memory_space=pl.ANY)] * len(arrays),
+        out_specs=(pl.BlockSpec(memory_space=pltpu.HBM),) * len(arrays),
+        scratch_shapes=[pltpu.SemaphoreType.DMA((len(arrays),))],
+        compiler_params=pltpu.CompilerParams(vmem_limit_bytes=1 * MiB),
+        name="settle",
+    )(*arrays)
 
 
 def shards(
@@ -672,6 +698,7 @@
         nz, nmp, ratio, kv_weight, prefix_hidden[0], norm_gain[None], level, prefix_lengths,
         action_query[0], action_kv[0], out_cotangent[0], prefix_blocks, action_blocks,
     )
+    attn_out, query_grad, d_action, summed = settle(attn_out, query_grad, d_action, summed)
     weight_grad = summed.reshape(depth, chunks, 2, HD).transpose(0, 2, 1, 3).reshape(depth, 2, columns)
     return (
         attn_out[None],

time: 164 us -> 162 us (0.988)
  local copies, waits for them, and re-layouts: 4.3 us -> 0 us
  Pallas kernels: 158 us -> 160 us
    unnamed x4 -> x0, local copies, waits for them, and re-layouts: 4.3 us -> none
    pallas_call x0 -> x1, Pallas kernels: none -> 2.48 us  [settle(): pl.pallas_call(settle_kernel, out_shape=tuple((jax.ShapeDtypeStruct(a.sha...]
where the time goes in v3:
time: 162 us
  Pallas kernels  160 us (99%)
  between operations  2.12 us (1%)
    pallas_call x1, Pallas kernels, fused(): pl.pallas_call(functools.partial(kernel, order, nz, nmp, ratio), out_shap...  157 us

profile of v3, /device:TPU:0, one launch (start us, length us, event | category | flops | bytes accessed | tf_op | source)
XLA Modules:
  0.0 162.1 jit_solution(2889161243893251136)
XLA Ops:
  1.9 157.5 %fused.1 = (bf16[128,1024]{1,0:T(8,128)(2,1)S(1)}, f32[128,1024]{1,0:T(8,128)S(1)}, f32[128,2,512]{2,1,0:T(2,128)S(1)}, f32[8192,128]{1,0:T(8,128)S(1)}) custom-call(bf16[1024,2,512]{2,1,0:T(2,128)(2,1)} %w_hbm.1, bf16[256,8192]{1,0:T(8,128)(2,1)} %bitcast.13, f32[1,8192]{1,0:T(1,128)} %bitcast.17, f32[1]{0:T(128)S(6)} %add.7.level_ref, ...), custom_call_target="tpu_custom_call" | custom-call | tf_op jit(solution)/shard_map/fused/pallas_call | solution.py:603
  159.4 2.5 %settle.1 = (bf16[128,1024]{1,0:T(8,128)(2,1)}, f32[128,1024]{1,0:T(8,128)}, f32[128,2,512]{2,1,0:T(2,128)}, f32[8192,128]{1,0:T(8,128)}) custom-call(bf16[128,1024]{1,0:T(8,128)(2,1)S(1)} %get-tuple-element.12.refs_0_, f32[128,1024]{1,0:T(8,128)S(1)} %get-tuple-element.13.refs_1_, f32[128,2,512]{2,1,0:T(2,128)S(1)} %get-tuple-element.14.refs_2_, ...), custom_call_target="tpu_custom_call" | custom-call | tf_op jit(solution)/shard_map/settle/pallas_call | solution.py:667

commit v4 on v3

--- a/solution.py
+++ b/solution.py
@@ -515,7 +515,10 @@
     def other_half(c):
         for i in range(cuts):
             o_copy(c, i).wait()
-        spread(c, 1 - seg, o_ref.at[c])
+            for kv in range(2):
+                first = ((1 - seg) * half + i * depth) * (2 * chunks) + c * 2 + kv
+                part = pl.ds(first, depth, stride=2 * chunks)
+                grad_ref[part, :] = o_ref[c, i * depth : (i + 1) * depth, kv * HD : (kv + 1) * HD].astype(jnp.float32)
 
     def clear():
         @pl.when(z == 0)

time: 162 us -> 162 us (level)
  no operation moved by 1% of the time
where the time goes in v4:
time: 162 us
  Pallas kernels  160 us (99%)
  between operations  2.12 us (1%)
    pallas_call x1, Pallas kernels, fused(): pl.pallas_call(functools.partial(kernel, order, nz, nmp, ratio), out_shap...  157 us

profile of v4, /device:TPU:0, one launch (start us, length us, event | category | flops | bytes accessed | tf_op | source)
XLA Modules:
  0.0 162.0 jit_solution(8965120072477352850)
XLA Ops:
  1.9 157.4 %fused.1 = (bf16[128,1024]{1,0:T(8,128)(2,1)S(1)}, f32[128,1024]{1,0:T(8,128)S(1)}, f32[128,2,512]{2,1,0:T(2,128)S(1)}, f32[8192,128]{1,0:T(8,128)S(1)}) custom-call(bf16[1024,2,512]{2,1,0:T(2,128)(2,1)} %w_hbm.1, bf16[256,8192]{1,0:T(8,128)(2,1)} %bitcast.13, f32[1,8192]{1,0:T(1,128)} %bitcast.17, f32[1]{0:T(128)S(6)} %add.7.level_ref, ...), custom_call_target="tpu_custom_call" | custom-call | tf_op jit(solution)/shard_map/fused/pallas_call | solution.py:606
  159.3 2.5 %settle.1 = (bf16[128,1024]{1,0:T(8,128)(2,1)}, f32[128,1024]{1,0:T(8,128)}, f32[128,2,512]{2,1,0:T(2,128)}, f32[8192,128]{1,0:T(8,128)}) custom-call(bf16[128,1024]{1,0:T(8,128)(2,1)S(1)} %get-tuple-element.12.refs_0_, f32[128,1024]{1,0:T(8,128)S(1)} %get-tuple-element.13.refs_1_, f32[128,2,512]{2,1,0:T(2,128)S(1)} %get-tuple-element.14.refs_2_, ...), custom_call_target="tpu_custom_call" | custom-call | tf_op jit(solution)/shard_map/settle/pallas_call | solution.py:670
